TPU v7x, 32 devices: a whole 2x2x4 slice. The times are simulated.
32 devices in a mesh: req: 4 (over x, core), mlp: 8 (over z, y).
Axes of the slice: x: 2, y: 2, z: 4, core: 2. Of those that a mesh axis runs over, the one named last changes fastest.
Arguments:
- resid: bfloat16 [4096, 3072], P(('req', 'mlp')), may hold values from -6 to 6
- queries: bfloat16 [4096, 1536], P(('req', 'mlp')), may hold values from -240 to 240
- fresh_keys: bfloat16 [4096, 256], P(('req', 'mlp')), may hold values from -6 to 6
- fresh_values: bfloat16 [4096, 256], P(('req', 'mlp')), may hold values from -6 to 6
- paged_key_cache: bfloat16 [64, 128, 256], P(('req', 'mlp')), may hold values from -6 to 6
- paged_value_cache: bfloat16 [64, 128, 256], P(('req', 'mlp')), may hold values from -6 to 6
- page_table: int32 [4, 16], P('req'), may hold values from 0 to 15, as said below
- cache_lengths: int32 [4], P('req'), may hold values from 1 to 2048, as said below
- out_weight: bfloat16 [1536, 3072], replicated, may hold values from -0.15625 to 0.15625
- norm_gain: float32 [3072], replicated, may hold values from 0.5 to 1.5
- gate_weight: bfloat16 [3072, 8192], P('req', 'mlp'), may hold values from -0.109375 to 0.109375
- up_weight: bfloat16 [3072, 8192], P('req', 'mlp'), may hold values from -0.109375 to 0.109375
- down_weight: bfloat16 [8192, 3072], P('mlp', 'req'), may hold values from -0.0625 to 0.0625
Outputs:
- layer_out: bfloat16 [4096, 3072], P(('req', 'mlp'))
Inputs may be any that keep to these rules, and one draw needn't show every extreme that they name: `page_table`: within the 1 request of one index of req the entries are a permutation of 0 to 15. `cache_lengths`: half of the requests hold at most 128 cached tokens, the other half more than 1920; some request holds exactly 2048.
All inputs are finite; a program needn't handle non-finite values.
Results may differ from a plain program's by a relative error of at most 0.0085.
Values may be sent and summed in bfloat16 or wider, within the bound.
A program may use at most 128 MiB of HBM per device.

v0:
```python
import jax
import jax.numpy as jnp
from jax import lax
from jax.sharding import PartitionSpec as P

QUERY_HEADS = 12
KEY_VALUE_HEADS = 2
HEAD_SIZE = 128
REQ_DEV = 1


def body(
    resid,
    queries,
    fresh_keys,
    fresh_values,
    paged_key_cache,
    paged_value_cache,
    page_table,
    cache_lengths,
    out_weight,
    norm_gain,
    gate_weight,
    up_weight,
    down_weight,
):
    token_position = queries.shape[0]
    group_ratio = QUERY_HEADS // KEY_VALUE_HEADS
    scale = HEAD_SIZE ** (-0.5)
    seq_len = token_position * lax.axis_size("mlp") // REQ_DEV
    place = lax.axis_index("mlp")
    first = place * token_position
    request = first // seq_len
    length = lax.dynamic_index_in_dim(cache_lengths, request, 0, keepdims=False)
    table_row = lax.dynamic_index_in_dim(page_table, request, 0, keepdims=False)
    heads_of_queries = queries.reshape(token_position, KEY_VALUE_HEADS, group_ratio, HEAD_SIZE)

    def update(state, joined_keys, joined_values, valid):
        peak, total, summed = state
        heads_of_keys = joined_keys.reshape(-1, KEY_VALUE_HEADS, HEAD_SIZE)
        heads_of_values = joined_values.reshape(-1, KEY_VALUE_HEADS, HEAD_SIZE)
        scores = (
            jnp.einsum(
                "tgrd,kgd->grtk",
                heads_of_queries,
                heads_of_keys,
                preferred_element_type=jnp.float32,
            )
            * scale
        )
        scores = jnp.where(valid, scores, -1e30)
        new_peak = jnp.maximum(peak, jnp.max(scores, axis=-1))
        expo = jnp.where(valid, jnp.exp(scores - new_peak[..., None]), 0.0)
        factor = jnp.exp(peak - new_peak)
        total = total * factor + jnp.sum(expo, axis=-1)
        summed = summed * factor[..., None] + jnp.einsum(
            "grtk,kgd->grtd",
            expo.astype(jnp.bfloat16),
            heads_of_values,
            preferred_element_type=jnp.float32,
        )
        return (new_peak, total, summed)

    state = (
        jnp.full((KEY_VALUE_HEADS, group_ratio, token_position), -1e30, jnp.float32),
        jnp.zeros((KEY_VALUE_HEADS, group_ratio, token_position), jnp.float32),
        jnp.zeros((KEY_VALUE_HEADS, group_ratio, token_position, HEAD_SIZE), jnp.float32),
    )
    rows_of_queries = first + jnp.arange(token_position, dtype=jnp.int32)
    rows_of_keys = lax.all_gather(fresh_keys, "mlp", axis=0, tiled=True)
    rows_of_values = lax.all_gather(fresh_values, "mlp", axis=0, tiled=True)
    count = rows_of_keys.shape[0]
    key_index = jnp.arange(count, dtype=jnp.int32)
    same = key_index[None, :] // seq_len == rows_of_queries[:, None] // seq_len
    valid = same & (key_index[None, :] <= rows_of_queries[:, None])
    state = update(state, rows_of_keys, rows_of_values, valid)
    key_page = lax.all_gather(paged_key_cache, "mlp", axis=0, tiled=True)
    value_page = lax.all_gather(paged_value_cache, "mlp", axis=0, tiled=True)
    count = key_page.shape[0]
    depth = key_page.shape[1]
    cache_positions = jnp.arange(count, dtype=jnp.int32)
    match = table_row[None, :] == cache_positions[:, None]
    owned = jnp.any(match, axis=1)
    page = jnp.sum(
        jnp.where(match, jnp.arange(table_row.shape[0], dtype=jnp.int32)[None, :], 0), axis=1
    )
    positions = page[:, None] * depth + jnp.arange(depth, dtype=jnp.int32)[None, :]
    live = (owned[:, None] & (positions < length)).reshape(1, count * depth)
    joined_keys = key_page.reshape(count * depth, -1)
    joined_values = value_page.reshape(count * depth, -1)
    state = update(state, joined_keys, joined_values, live)
    peak, total, summed = state
    attended = summed / total[..., None]
    attn = (
        jnp.transpose(attended, (2, 0, 1, 3))
        .reshape(token_position, QUERY_HEADS * HEAD_SIZE)
        .astype(jnp.bfloat16)
    )
    h = resid.astype(jnp.float32) + jnp.dot(attn, out_weight, preferred_element_type=jnp.float32)
    normed = (h * lax.rsqrt(jnp.mean(h * h, axis=-1, keepdims=True) + 1e-05) * norm_gain).astype(
        jnp.bfloat16
    )
    whole = lax.all_gather(normed, "mlp", axis=0, tiled=True)

    def add_rows(piece):
        return jnp.dot(whole, piece, preferred_element_type=jnp.float32)

    gate = add_rows(lax.all_gather(gate_weight, "req", axis=0, tiled=True))
    upper = add_rows(lax.all_gather(up_weight, "req", axis=0, tiled=True))
    hidden = (jax.nn.silu(gate) * upper).astype(jnp.bfloat16)
    terms = jnp.dot(
        hidden,
        lax.all_gather(down_weight, "req", axis=1, tiled=True),
        preferred_element_type=jnp.float32,
    )
    mixed = lax.psum_scatter(
        terms.astype(jnp.bfloat16), "mlp", scatter_dimension=0, tiled=True
    ).astype(jnp.float32)
    return (h + mixed).astype(jnp.bfloat16)


def solution(mesh):
    placed = (
        P(("req", "mlp"), None),
        P(("req", "mlp"), None),
        P(("req", "mlp"), None),
        P(("req", "mlp"), None),
        P(("req", "mlp"), None, None),
        P(("req", "mlp"), None, None),
        P("req", None),
        P("req"),
        P(),
        P(),
        P("req", "mlp"),
        P("req", "mlp"),
        P("mlp", "req"),
    )
    return jax.shard_map(
        body, mesh=mesh, in_specs=placed, out_specs=P(("req", "mlp"), None), check_vma=False
    )
```

profile of v0, /device:TPU:0, one launch (start us, length us, event | category | flops | bytes accessed | tf_op | source)
XLA Modules:
  0.0 476.9 jit_solution(3383910963019407040)
XLA Ops:
  6.5 0.0 all-gather.7.cloned.1.call-start
  6.5 0.7 all-gather.7.cloned.1.call-update
  7.3 0.0 all-gather.9.cloned.1.call-start
  7.3 0.7 all-gather.9.cloned.1.call-update
  8.0 0.0 all-gather.13.cloned.1.call-start
  8.1 0.7 all-gather.13.cloned.1.call-update
  8.7 0.0 all-gather.11.cloned.1.call-start
  9.4 1.2 copy.43
  10.7 1.0 copy.42
  11.6 34.4 %all_gather.25 = bf16[1024,256]{1,0:T(8,128)(2,1)S(1)} all-gather(bf16[128,256]{1,0:T(8,128)(2,1)} %param.16), channel_id=1, replica_groups=mesh['req'=4,'mlp'=8] {'mlp'}, dimensions={0}, use_global_device_ids=true | all-gather | bytes 589824 | tf_op jit(solution)/shard_map/all_gather | solution.py:71
  46.0 1.0 copy.46
  47.0 0.8 fusion.47
  47.8 0.8 select_reduce_fusion
  48.6 0.1 fusion.49
  48.7 0.2 fusion.42
  48.9 0.0 copy-start
  48.9 28.2 %all_gather.24 = bf16[1024,256]{0,1:T(8,128)(2,1)S(1)} all-gather(bf16[128,256]{0,1:T(8,128)(2,1)S(1)} %copy.42), channel_id=1, replica_groups=mesh['req'=4,'mlp'=8] {'mlp'}, dimensions={0}, use_global_device_ids=true | all-gather | bytes 589824 | tf_op jit(solution)/shard_map/all_gather | solution.py:70
  77.1 0.0 copy-done
  77.1 3.8 fusion.8
  80.9 0.0 all-gather.7.cloned.1.call-done
  80.9 1.4 reshape.148
  82.4 14.6 %all-gather.9.cloned.1.call-done = bf16[16,128,256]{2,1,0:T(8,128)(2,1)} async-done(((bf16[2,128,256]{2,1,0:T(8,128)(2,1)}), bf16[16,128,256]{2,1,0:T(8,128)(2,1)}) %all-gather.9.cloned.1.call-update) | async-done | bytes 1048592 | tf_op jit(solution)/shard_map/all_gather | solution.py:78
  97.0 0.0 slice-start
  97.0 2.4 reshape.149
  99.3 1.9 bitcast_reduce_fusion
  101.3 0.0 slice-done
  101.3 0.2 slice-done.1
  101.5 0.0 copy-done.1
  101.5 1.5 fusion.9
  103.0 0.0 copy-start.4
  103.1 3.8 fusion.2
  106.9 0.0 copy-done.4
  106.9 0.0 copy-start.2
  106.9 0.0 slice-start.2
  106.9 1.7 fusion.26
  108.6 0.0 copy-done.2
  108.6 0.0 slice-start.3
  108.6 0.0 slice-start.4
  108.6 0.0 copy-start.3
  108.6 3.4 fusion.37
  112.0 0.0 slice-done.2
  112.0 0.0 slice-done.3
  112.0 0.0 slice-done.4
  112.0 0.0 copy-done.3
  112.0 0.0 copy-start.5
  112.1 1.6 multiply_reduce_fusion
  113.6 0.0 copy-done.5
  113.6 1.1 multiply_convert_fusion.1
  114.8 0.0 all-gather.11.cloned.1.call-update
  114.8 0.0 all-gather.15.cloned.1.call-start
  114.8 0.5 all-gather.15.cloned.1.call-update
  115.4 0.0 all-gather.17.cloned.1.call-start
  115.4 0.5 all-gather.17.cloned.1.call-update
  115.9 0.0 reduce-scatter.2.cloned.1.call-start
  116.0 27.7 %all-gather.13.cloned.1.call-done = bf16[3072,1024]{1,0:T(8,128)(2,1)} async-done(((bf16[768,1024]{1,0:T(8,128)(2,1)}), bf16[3072,1024]{1,0:T(8,128)(2,1)}) %all-gather.13.cloned.1.call-update) | async-done | bytes 6291472 | tf_op jit(solution)/shard_map/all_gather | solution.py:108
  143.7 101.1 %all-gather.11.cloned.1.call-done = bf16[1024,3072]{1,0:T(8,128)(2,1)} async-done(((bf16[128,3072]{1,0:T(8,128)(2,1)}), bf16[1024,3072]{1,0:T(8,128)(2,1)}) %all-gather.11.cloned.1.call-update) | async-done | bytes 6291472 | tf_op jit(solution)/shard_map/all_gather | solution.py:103
  244.8 11.9 %fusion.61 = f32[1024,1024]{1,0:T(8,128)} fusion(bf16[1024,3072]{1,0:T(8,128)(2,1)} %all-gather.11.cloned.1.call-done, bf16[3072,1024]{1,0:T(8,128)(2,1)} %all-gather.13.cloned.1.call-done), kind=kOutput, calls=%fused_computation.71 | convolution fusion | flops 6442450944 | bytes 16777216 | tf_op jit(solution)/shard_map/dot_general | solution.py:106
  256.8 34.1 %all-gather.15.cloned.1.call-done = bf16[3072,1024]{1,0:T(8,128)(2,1)} async-done(((bf16[768,1024]{1,0:T(8,128)(2,1)}), bf16[3072,1024]{1,0:T(8,128)(2,1)}) %all-gather.15.cloned.1.call-update) | async-done | bytes 6291472 | tf_op jit(solution)/shard_map/all_gather | solution.py:109
  290.8 12.7 %multiply_convert_fusion = bf16[1024,1024]{1,0:T(8,128)(2,1)} fusion(f32[1024,1024]{1,0:T(8,128)} %fusion.61, bf16[1024,3072]{1,0:T(8,128)(2,1)} %all-gather.11.cloned.1.call-done, bf16[3072,1024]{1,0:T(8,128)(2,1)} %all-gather.15.cloned.1.call-done), kind=kOutput, calls=%fused_computation.16 | convolution fusion | flops 6448742400 | bytes 18874368 | tf_op jit(solution)/shard_map/dot_general | solution.py:106
  303.5 35.1 %all-gather.17.cloned.1.call-done = bf16[1024,3072]{1,0:T(8,128)(2,1)} async-done(((bf16[1024,768]{1,0:T(8,128)(2,1)}), bf16[1024,3072]{1,0:T(8,128)(2,1)}) %all-gather.17.cloned.1.call-update) | async-done | bytes 6291472 | tf_op jit(solution)/shard_map/all_gather | solution.py:113
  338.7 11.1 %convolution_convert_fusion = bf16[1024,3072]{1,0:T(8,128)(2,1)} fusion(bf16[1024,1024]{1,0:T(8,128)(2,1)} %multiply_convert_fusion, bf16[1024,3072]{1,0:T(8,128)(2,1)} %all-gather.17.cloned.1.call-done), kind=kOutput, calls=%fused_computation.12 | convolution fusion | flops 6445596672 | bytes 14680064 | tf_op jit(solution)/shard_map/dot_general | solution.py:111
  349.8 0.0 reduce-scatter.2.cloned.1.call-update
  349.8 118.1 %reduce-scatter.2.cloned.1.call-done = bf16[128,3072]{1,0:T(8,128)(2,1)} async-done(((bf16[1024,3072]{1,0:T(8,128)(2,1)}), bf16[128,3072]{1,0:T(8,128)(2,1)}) %reduce-scatter.2.cloned.1.call-update) | async-done | bytes 786448 | tf_op jit(solution)/shard_map/reduce_scatter | solution.py:116
  467.8 2.2 add_convert_fusion
  (10 shorter events, 0.1 us)
Async XLA Ops:
  6.5 74.4 %all-gather.7.cloned.1.call-start = ((), (), s32[]{:S(2)}) async-start(), calls=%async_computation.1 | async-start | bytes 1179648 | tf_op jit(solution)/shard_map/all_gather | solution.py:77
  7.3 89.7 %all-gather.9.cloned.1.call-start = ((), (), s32[]{:S(2)}) async-start(), calls=%async_computation.2 | async-start | bytes 1179648 | tf_op jit(solution)/shard_map/all_gather | solution.py:78
  8.0 135.7 %all-gather.13.cloned.1.call-start = ((), (), s32[]{:S(2)}) async-start(), calls=%async_computation.4 | async-start | bytes 7864320 | tf_op jit(solution)/shard_map/all_gather | solution.py:108
  8.7 236.1 %all-gather.11.cloned.1.call-start = ((), (), s32[]{:S(2)}) async-start(), calls=%async_computation.3 | async-start | bytes 7077888 | tf_op jit(solution)/shard_map/all_gather | solution.py:103
  48.9 28.2 %copy-start = (pred[128,1024]{0,1:T(8,128)(4,1)}, pred[128,1024]{0,1:T(8,128)(4,1)S(1)}, u32[]{:S(2)}) copy-start(pred[128,1024]{0,1:T(8,128)(4,1)S(1)} %fusion.42) | copy-start | bytes 393220
  97.0 4.3 slice-start
  99.3 2.2 slice-start.1
  99.3 2.2 copy-start.1
  103.0 3.8 copy-start.4
  106.9 1.7 copy-start.2
  106.9 5.1 %slice-start.2 = ((s8[9437184]{0:T(1024)(128)(4,1)}), s8[4194304]{0:T(1024)(128)(4,1)S(1)}, s32[]{:S(2)}) async-start(s8[9437184]{0:T(1024)(128)(4,1)} %bitcast.105), calls=%async_computation.10 | async-start | bytes 8388608
  108.6 3.4 slice-start.3
  108.6 3.4 slice-start.4
  108.6 3.4 copy-start.3
  112.0 1.6 copy-start.5
  114.8 176.0 %all-gather.15.cloned.1.call-start = ((), (), s32[]{:S(2)}) async-start(), calls=%async_computation.5 | async-start | bytes 7864320 | tf_op jit(solution)/shard_map/all_gather | solution.py:109
  115.4 223.3 %all-gather.17.cloned.1.call-start = ((), (), s32[]{:S(2)}) async-start(), calls=%async_computation.6 | async-start | bytes 7864320 | tf_op jit(solution)/shard_map/all_gather | solution.py:113
  115.9 351.9 %reduce-scatter.2.cloned.1.call-start = ((), (), s32[]{:S(2)}) async-start(), calls=%async_computation.7 | async-start | bytes 7077888 | tf_op jit(solution)/shard_map/reduce_scatter | solution.py:116
Sparse Core Ops, SparseCore 0:
  9.5 44.9 all-gather.6
  56.6 40.3 all-gather.8
  98.5 45.1 all-gather.12
  145.7 99.0 all-gather.10
  246.2 44.5 all-gather.14
  292.2 46.3 all-gather.16
  349.9 117.9 reduce-scatter.1
where the time goes:
time: 477 us
  waiting for transfers between devices  334 us (70%)
  blocking collectives  62.6 us (13%)
  matrix products  48.1 us (10%)
  between operations  14.4 us (3%)
  other arithmetic  10.4 us (2%)
  local copies, waits for them, and re-layouts  7.24 us (2%)
    reduce_scatter x1, waiting for transfers between devices, body(): lax.psum_scatter(terms.astype(jnp.bfloat16), 'mlp', scatter_dimension=0,...  118 us
    all_gather x1, waiting for transfers between devices, body(): whole = lax.all_gather(normed, 'mlp', axis=0, tiled=True)  101 us
    all_gather x1, waiting for transfers between devices, body(): lax.all_gather(down_weight, 'req', axis=1, tiled=True)  35.1 us
    all_gather x1, blocking collectives, body(): rows_of_values = lax.all_gather(fresh_values, 'mlp', axis=0, tiled=True)  34.4 us
    all_gather x1, waiting for transfers between devices, body(): upper = add_rows(lax.all_gather(up_weight, 'req', axis=0, tiled=True))  34.1 us
    all_gather x1, blocking collectives, body(): rows_of_keys = lax.all_gather(fresh_keys, 'mlp', axis=0, tiled=True)  28.2 us
    all_gather x1, waiting for transfers between devices, body(): gate = add_rows(lax.all_gather(gate_weight, 'req', axis=0, tiled=True))  27.7 us
    dot_general x2, matrix products, add_rows(): return jnp.dot(whole, piece, preferred_element_type=jnp.float32)  24.7 us
  transfers between devices with their start and end apart: 7, of which 6 were waited for; matrix products, arithmetic and copies ran while one was open for 11% of the time, Pallas kernels for 0%

commit v1 on v0

v1 whole, which is shorter than its diff:
```python
import functools
import math

import jax
import jax.numpy as jnp
from jax import lax
from jax.experimental import pallas as pl
from jax.experimental.pallas import tpu as pltpu
from jax.sharding import PartitionSpec as P

QUERY_HEADS = 12
KEY_VALUE_HEADS = 2
HEAD_SIZE = 128
GROUP = QUERY_HEADS // KEY_VALUE_HEADS
KV_COLS = KEY_VALUE_HEADS * HEAD_SIZE
MESH = pl.DeviceIdType.MESH


def flip(a, k):
    bit = 1
    while bit <= k:
        if k & bit:
            a = a + bit - 2 * bit * (lax.rem(a // bit, 2))
        bit *= 2
    return a


def kernel(
    n, nr,
    q_ref, resid_ref, pos_ref, gain_ref, fk, fv, pk, pv, ow, wg, wu, wd,
    out_ref,
    kv, nrm, wgs, wus, wds, big, yrecv, zrecv, h, attn, bias, hid,
    loc, kv_send, kv_fwd, kv_recv, n_send, n_fwd, n_recv,
    w_send, w_fwd, w_recv, y_send, y_recv, z_send, z_recv,
):
    A, X = n // 2, nr // 2
    me, r = lax.axis_index("mlp"), lax.axis_index("req")
    a, b = me // 2, lax.rem(me, 2)
    x, c = r // 2, lax.rem(r, 2)
    partner, sibling = a * 2 + 1 - b, x * 2 + 1 - c
    T, D = resid_ref.shape
    cached = pk.shape[0]
    R = cached + T
    depth = wg.shape[0]
    F = wg.shape[1]
    Dq = wd.shape[1]

    def peer(k):
        return flip(a, k) * 2 + b

    def rpeer(k):
        return flip(x, k) * 2 + c

    def remote(src, dst, ss, rs, axis, idx):
        return pltpu.make_async_remote_copy(
            src_ref=src, dst_ref=dst, send_sem=ss, recv_sem=rs,
            device_id={axis: idx}, device_id_type=MESH,
        )

    def kv_slot(s):
        return kv.at[pl.ds(pl.multiple_of(s * R, 128), R), :]

    def n_slot(s):
        return nrm.at[pl.ds(pl.multiple_of(s * T, 128), T), :]

    def w_slot(i, s):
        if i == 2:
            return wds.at[s]
        buf = wgs if i == 0 else wus
        return buf.at[pl.ds(pl.multiple_of(s * depth, 128), depth), :]

    weights = (wg, wu, wd)

    base = pl.multiple_of(me * R, 128)
    mine = [
        pltpu.make_async_copy(pk, kv.at[pl.ds(base, cached), pl.ds(0, KV_COLS)], loc.at[0]),
        pltpu.make_async_copy(pv, kv.at[pl.ds(base, cached), pl.ds(KV_COLS, KV_COLS)], loc.at[1]),
        pltpu.make_async_copy(fk, kv.at[pl.ds(base + cached, T), pl.ds(0, KV_COLS)], loc.at[2]),
        pltpu.make_async_copy(fv, kv.at[pl.ds(base + cached, T), pl.ds(KV_COLS, KV_COLS)], loc.at[3]),
    ]
    own_ow = pltpu.make_async_copy(ow, big.at[pl.ds(0, ow.shape[0]), :], loc.at[4])
    own_w = [pltpu.make_async_copy(weights[i], w_slot(i, r), loc.at[5 + i]) for i in range(3)]
    for copy in mine:
        copy.start()

    barrier = pltpu.get_barrier_semaphore()
    pl.semaphore_signal(barrier, inc=1, device_id={"mlp": partner}, device_id_type=MESH)
    pl.semaphore_signal(barrier, inc=1, device_id={"req": sibling}, device_id_type=MESH)
    for k in range(1, A):
        pl.semaphore_signal(barrier, inc=1, device_id={"mlp": peer(k)}, device_id_type=MESH)
    for k in range(1, X):
        pl.semaphore_signal(barrier, inc=1, device_id={"req": rpeer(k)}, device_id_type=MESH)
    for copy in mine:
        copy.wait()
    pl.semaphore_wait(barrier, A + X)

    started = []

    def send(copy):
        copy.start()
        started.append(copy)

    def spread(slot, send_sem, recv_sem):
        src = slot(me)
        for k in range(1, A):
            send(remote(src, slot(me), send_sem.at[k], recv_sem.at[me], "mlp", peer(k)))
        send(remote(src, slot(me), send_sem.at[0], recv_sem.at[me], "mlp", partner))

    def arrived(slot, s, recv_sem, send_sem):
        remote(slot(s), slot(s), send_sem.at[0], recv_sem.at[s], "mlp", partner).wait_recv()

    def forward(k, slot, recv_sem, fwd_sem):
        s = peer(k)
        arrived(slot, s, recv_sem, fwd_sem)
        send(remote(slot(s), slot(s), fwd_sem.at[k], recv_sem.at[s], "mlp", partner))

    def other(k):
        return flip(a, k) * 2 + 1 - b

    spread(kv_slot, kv_send, kv_recv)
    for i in range(3):
        for k in range(1, X):
            send(remote(weights[i], w_slot(i, r), w_send.at[i, k], w_recv.at[i, r], "req", rpeer(k)))
    for i in range(3):
        send(remote(weights[i], w_slot(i, r), w_send.at[i, 0], w_recv.at[i, r], "req", sibling))
    own_ow.start()
    for copy in own_w:
        copy.start()

    def forward_weight(i):
        for k in range(1, X):
            s = rpeer(k)
            remote(w_slot(i, s), w_slot(i, s), w_fwd.at[i, k], w_recv.at[i, s], "req", sibling).wait_recv()
            send(remote(w_slot(i, s), w_slot(i, s), w_fwd.at[i, k], w_recv.at[i, s], "req", sibling))

    def weight_arrived(i):
        own_w[i].wait()
        for k in range(X):
            s = flip(x, k) * 2 + 1 - c
            remote(w_slot(i, s), w_slot(i, s), w_fwd.at[i, 0], w_recv.at[i, s], "req", sibling).wait_recv()

    rows = lax.broadcasted_iota(jnp.int32, (T, n * R), 0) + me * T
    bias[...] = jnp.where(pos_ref[...] <= rows, 0.0, -1e30)
    for k in range(1, A):
        forward(k, kv_slot, kv_recv, kv_fwd)
    for k in range(A):
        arrived(kv_slot, other(k), kv_recv, kv_fwd)

    factor = HEAD_SIZE ** (-0.5) * math.log2(math.e)

    def attend(i, carry):
        head = 2 * i
        g = head // GROUP
        first = pl.multiple_of(head * HEAD_SIZE, 128)
        second = pl.multiple_of(head * HEAD_SIZE + HEAD_SIZE, 128)
        qq = jnp.concatenate(
            [q_ref[:, pl.ds(first, HEAD_SIZE)], q_ref[:, pl.ds(second, HEAD_SIZE)]], axis=0
        )
        keys = kv[:, pl.ds(pl.multiple_of(g * HEAD_SIZE, 128), HEAD_SIZE)]
        values = kv[:, pl.ds(pl.multiple_of(KV_COLS + g * HEAD_SIZE, 128), HEAD_SIZE)]
        s = lax.dot_general(qq, keys, (((1,), (1,)), ((), ())), preferred_element_type=jnp.float32)
        s = (s * factor).reshape(2, T, n * R) + bias[...][None]
        e = jnp.exp2(s - jnp.max(s, axis=-1, keepdims=True))
        total = jnp.sum(e, axis=-1, keepdims=True)
        o = jnp.dot(
            e.astype(jnp.bfloat16).reshape(2 * T, n * R), values, preferred_element_type=jnp.float32
        ).reshape(2, T, HEAD_SIZE) / total
        attn[:, pl.ds(first, HEAD_SIZE)] = o[0].astype(jnp.bfloat16)
        attn[:, pl.ds(second, HEAD_SIZE)] = o[1].astype(jnp.bfloat16)
        return carry

    lax.fori_loop(0, QUERY_HEADS // 2, attend, 0)

    own_ow.wait()

    def project(j, squares):
        cols = pl.ds(pl.multiple_of(j * 256, 256), 256)
        piece = resid_ref[:, cols].astype(jnp.float32) + jnp.dot(
            attn[...], big[pl.ds(0, QUERY_HEADS * HEAD_SIZE), cols], preferred_element_type=jnp.float32
        )
        h[:, cols] = piece
        return squares + jnp.sum(piece * piece, axis=-1, keepdims=True)

    squares = lax.fori_loop(0, D // 256, project, jnp.zeros((T, 1), jnp.float32))
    inverse = lax.rsqrt(squares / D + 1e-05)
    nrm[pl.ds(pl.multiple_of(me * T, 128), T), :] = (h[...] * inverse * gain_ref[...]).astype(jnp.bfloat16)
    spread(n_slot, n_send, n_recv)

    width = 256 if Dq % 256 == 0 else 128

    def feed(ap):
        pair = pl.ds(pl.multiple_of(ap * 2 * T, 256), 2 * T)

        def gated(j, carry):
            cols = pl.ds(pl.multiple_of(j * 256, 256), 256)
            gate = jnp.dot(nrm[pair, :], wgs[:, cols], preferred_element_type=jnp.float32)
            upper = jnp.dot(nrm[pair, :], wus[:, cols], preferred_element_type=jnp.float32)
            hid[:, cols] = (gate / (1.0 + jnp.exp(-gate)) * upper).astype(jnp.bfloat16)
            return carry

        lax.fori_loop(0, F // 256, gated, 0)

        def lowered(s, carry):
            for j in range(Dq // width):
                piece = jnp.dot(
                    hid[...], wds[s, :, j * width : (j + 1) * width], preferred_element_type=jnp.float32
                )
                cols = pl.ds(pl.multiple_of(s * Dq + j * width, 128), width)
                big[pair, cols] = piece.astype(jnp.bfloat16)
            return carry

        lax.fori_loop(0, nr, lowered, 0)

    def p_slot(s):
        return pl.ds(pl.multiple_of(s * T, 128), T)

    def y_copy(k):
        return remote(big.at[p_slot(other(k)), :], yrecv.at[k], y_send.at[k], y_recv.at[k], "mlp", partner)

    def z_copy(k):
        return remote(big.at[p_slot(peer(k)), :], zrecv.at[k - 1], z_send.at[k], z_recv.at[k], "mlp", peer(k))

    def combine(k):
        y_copy(k).wait_recv()
        rows = p_slot(peer(k))
        big[rows, :] = (big[rows, :].astype(jnp.float32) + yrecv[k].astype(jnp.float32)).astype(jnp.bfloat16)
        send(z_copy(k))

    forward_weight(0)
    forward_weight(1)
    if A > 1:
        forward(1, n_slot, n_recv, n_fwd)
    forward_weight(2)
    for i in range(3):
        weight_arrived(i)
    for k in range(A):
        arrived(n_slot, other(k), n_recv, n_fwd)
        feed(flip(a, k))
        send(y_copy(k))
        if k + 2 < A:
            forward(k + 2, n_slot, n_recv, n_fwd)
        if k >= 2:
            combine(k - 1)
    if A > 1:
        combine(A - 1)
    y_copy(0).wait_recv()
    h[...] = h[...] + (big[p_slot(me), :].astype(jnp.float32) + yrecv[0].astype(jnp.float32))
    for k in range(1, A):
        z_copy(k).wait_recv()
        h[...] = h[...] + zrecv[k - 1].astype(jnp.float32)
    out_ref[...] = h[...].astype(jnp.bfloat16)
    for copy in started:
        copy.wait_send()


def body(
    n, nr,
    resid, queries, fresh_keys, fresh_values, paged_key_cache, paged_value_cache,
    page_table, cache_lengths, out_weight, norm_gain, gate_weight, up_weight, down_weight,
):
    T, D = resid.shape
    own_pages, page_tokens = paged_key_cache.shape[:2]
    cached = own_pages * page_tokens
    R = cached + T
    A, X = n // 2, nr // 2
    slots = jnp.arange(n * own_pages, dtype=jnp.int32)
    match = page_table[0][None, :] == slots[:, None]
    page = jnp.sum(jnp.where(match, jnp.arange(page_table.shape[1], dtype=jnp.int32)[None, :], 0), axis=1)
    positions = page[:, None] * page_tokens + jnp.arange(page_tokens, dtype=jnp.int32)[None, :]
    live = jnp.any(match, axis=1)[:, None] & (positions < cache_lengths[0])
    stored = jnp.where(live, -1, 2**30).reshape(n, cached)
    fresh = jnp.arange(n * T, dtype=jnp.int32).reshape(n, T)
    pos = jnp.concatenate([stored, fresh], axis=1).reshape(1, n * R)
    depth, F = gate_weight.shape
    Dq = down_weight.shape[1]
    bf16, f32 = jnp.bfloat16, jnp.float32
    dma = pltpu.SemaphoreType.DMA
    vmem = pl.BlockSpec(memory_space=pltpu.VMEM)
    hbm = pl.BlockSpec(memory_space=pl.ANY)
    return pl.pallas_call(
        functools.partial(kernel, n, nr),
        out_shape=jax.ShapeDtypeStruct((T, D), bf16),
        in_specs=[vmem] * 4 + [hbm] * 8,
        out_specs=vmem,
        scratch_shapes=[
            pltpu.VMEM((n * R, 2 * KV_COLS), bf16),
            pltpu.VMEM((n * T, D), bf16),
            pltpu.VMEM((nr * depth, F), bf16),
            pltpu.VMEM((nr * depth, F), bf16),
            pltpu.VMEM((nr, F, Dq), bf16),
            pltpu.VMEM((max(n * T, out_weight.shape[0]), D), bf16),
            pltpu.VMEM((A, T, D), bf16),
            pltpu.VMEM((A - 1, T, D), bf16),
            pltpu.VMEM((T, D), f32),
            pltpu.VMEM((T, QUERY_HEADS * HEAD_SIZE), bf16),
            pltpu.VMEM((T, n * R), f32),
            pltpu.VMEM((2 * T, F), bf16),
            dma((8,)),
            dma((A,)), dma((A,)), dma((n,)),
            dma((A,)), dma((A,)), dma((n,)),
            dma((3, X)), dma((3, X)), dma((3, nr)),
            dma((A,)), dma((A,)), dma((A,)), dma((A,)),
        ],
        compiler_params=pltpu.CompilerParams(
            collective_id=0, has_side_effects=True, vmem_limit_bytes=62 * 2**20
        ),
    )(
        queries, resid, pos, norm_gain.reshape(1, D), fresh_keys, fresh_values,
        paged_key_cache.reshape(cached, KV_COLS), paged_value_cache.reshape(cached, KV_COLS),
        out_weight, gate_weight, up_weight, down_weight,
    )


def solution(mesh):
    placed = (
        P(("req", "mlp"), None),
        P(("req", "mlp"), None),
        P(("req", "mlp"), None),
        P(("req", "mlp"), None),
        P(("req", "mlp"), None, None),
        P(("req", "mlp"), None, None),
        P("req", None),
        P("req"),
        P(),
        P(),
        P("req", "mlp"),
        P("req", "mlp"),
        P("mlp", "req"),
    )
    return jax.shard_map(
        functools.partial(body, mesh.shape["mlp"], mesh.shape["req"]),
        mesh=mesh, in_specs=placed, out_specs=P(("req", "mlp"), None), check_vma=False,
    )
```

time: 477 us -> 279 us (0.58)
  the two profiles are of different devices: /device:TPU:0 before, /device:TPU:9 now
where the time goes in v1:
time: 279 us
  Pallas kernels  274 us (98%)
  local copies, waits for them, and re-layouts  3.04 us (1%)
    pallas_call x1, Pallas kernels, body(): pl.pallas_call(functools.partial(kernel, n, nr), out_shape=jax.ShapeDtype...  274 us

profile of v1, /device:TPU:9, one launch (start us, length us, event | category | flops | bytes accessed | tf_op | source)
XLA Modules:
  0.0 278.9 jit_solution(5123840995270661273)
XLA Ops:
  0.7 0.8 select_reduce_fusion
  1.4 0.8 fusion.1
  2.2 0.1 and.13
  2.3 0.1 copy.18
  2.4 0.1 mul.12
  2.5 0.1 copy.19
  2.6 0.1 fusion.3
  2.6 0.6 copy.20
  3.3 273.6 %shard_map.127 = bf16[128,3072]{1,0:T(8,128)(2,1)} custom-call(bf16[128,1536]{1,0:T(8,128)(2,1)} %q_ref.1, bf16[128,3072]{1,0:T(8,128)(2,1)} %resid_ref.1, s32[1,3072]{1,0:T(1,128)} %bitcast.24, f32[1,3072]{1,0:T(1,128)} %bitcast.25, bf16[128,256]{1,0:T(8,128)(2,1)} %fk.1, bf16[128,256]{1,0:T(8,128)(2,1)} %fv.1, bf16[256,256]{1,0:T(8,128)(2,1)} %bitcast.22, ...), custom_call_target="tpu_custom_call" | custom-call | tf_op jit(solution)/shard_map/pallas_call | solution.py:280
  276.9 2.1 copy.23
  (4 shorter events, 0.0 us)

commit v2 on v1

--- a/solution.py
+++ b/solution.py
@@ -25,12 +25,26 @@
     return a
 
 
+def at_least(u, v):
+    return (u - v + 1024) // 1024
+
+
+def nearest(a, count, j):
+    if j == 0:
+        return a
+    low = 1 - at_least(a, count // 2)
+    room = low * a + (1 - low) * (count - 1 - a)
+    both = at_least(2 * room, j)
+    step = (j + 1) // 2
+    return a + both * (-step if j % 2 else step) + (1 - both) * (2 * low - 1) * (j - room)
+
+
 def kernel(
     n, nr,
     q_ref, resid_ref, pos_ref, gain_ref, fk, fv, pk, pv, ow, wg, wu, wd,
     out_ref,
     kv, nrm, wgs, wus, wds, big, yrecv, zrecv, h, attn, bias, hid,
-    loc, kv_send, kv_fwd, kv_recv, n_send, n_fwd, n_recv,
+    loc, kv_send, kv_line, kv_recv, n_send, n_line, n_recv,
     w_send, w_fwd, w_recv, y_send, y_recv, z_send, z_recv,
 ):
     A, X = n // 2, nr // 2
@@ -46,7 +60,7 @@
     Dq = wd.shape[1]
 
     def peer(k):
-        return flip(a, k) * 2 + b
+        return nearest(a, A, k) * 2 + b
 
     def rpeer(k):
         return flip(x, k) * 2 + c
@@ -96,28 +110,39 @@
 
     started = []
 
-    def send(copy):
-        copy.start()
-        started.append(copy)
-
-    def spread(slot, send_sem, recv_sem):
-        src = slot(me)
-        for k in range(1, A):
-            send(remote(src, slot(me), send_sem.at[k], recv_sem.at[me], "mlp", peer(k)))
-        send(remote(src, slot(me), send_sem.at[0], recv_sem.at[me], "mlp", partner))
-
-    def arrived(slot, s, recv_sem, send_sem):
-        remote(slot(s), slot(s), send_sem.at[0], recv_sem.at[s], "mlp", partner).wait_recv()
-
-    def forward(k, slot, recv_sem, fwd_sem):
+    def send(copy, when=None):
+        started.append((copy, when))
+        if when is None:
+            copy.start()
+        else:
+            pl.when(when)(copy.start)
+
+    def along(slot, s, to, sem, recv_sem):
+        copy = remote(slot(s), slot(s), sem, recv_sem.at[s], "mlp", to * 2 + b)
+        send(copy, (to >= 0) & (to < A))
+
+    def across(slot, s, sem, recv_sem):
+        send(remote(slot(s), slot(s), sem, recv_sem.at[s], "mlp", partner))
+
+    def spread(slot, send_sem, line_sem, recv_sem):
+        along(slot, me, a + 1, line_sem.at[0], recv_sem)
+        along(slot, me, a - 1, line_sem.at[A], recv_sem)
+        across(slot, me, send_sem.at[0], recv_sem)
+
+    def arrived(slot, s, recv_sem):
+        remote(slot(s), slot(s), recv_sem.at[s], recv_sem.at[s], "mlp", partner).wait_recv()
+
+    def forward(k, slot, send_sem, line_sem, recv_sem):
         s = peer(k)
-        arrived(slot, s, recv_sem, fwd_sem)
-        send(remote(slot(s), slot(s), fwd_sem.at[k], recv_sem.at[s], "mlp", partner))
+        arrived(slot, s, recv_sem)
+        right = at_least(a, nearest(a, A, k))
+        along(slot, s, a + 2 * right - 1, line_sem.at[k], recv_sem)
+        across(slot, s, send_sem.at[k], recv_sem)
 
     def other(k):
-        return flip(a, k) * 2 + 1 - b
-
-    spread(kv_slot, kv_send, kv_recv)
+        return nearest(a, A, k) * 2 + 1 - b
+
+    spread(kv_slot, kv_send, kv_line, kv_recv)
     for i in range(3):
         for k in range(1, X):
             send(remote(weights[i], w_slot(i, r), w_send.at[i, k], w_recv.at[i, r], "req", rpeer(k)))
@@ -142,9 +167,9 @@
     rows = lax.broadcasted_iota(jnp.int32, (T, n * R), 0) + me * T
     bias[...] = jnp.where(pos_ref[...] <= rows, 0.0, -1e30)
     for k in range(1, A):
-        forward(k, kv_slot, kv_recv, kv_fwd)
+        forward(k, kv_slot, kv_send, kv_line, kv_recv)
     for k in range(A):
-        arrived(kv_slot, other(k), kv_recv, kv_fwd)
+        arrived(kv_slot, other(k), kv_recv)
 
     factor = HEAD_SIZE ** (-0.5) * math.log2(math.e)
 
@@ -184,7 +209,7 @@
     squares = lax.fori_loop(0, D // 256, project, jnp.zeros((T, 1), jnp.float32))
     inverse = lax.rsqrt(squares / D + 1e-05)
     nrm[pl.ds(pl.multiple_of(me * T, 128), T), :] = (h[...] * inverse * gain_ref[...]).astype(jnp.bfloat16)
-    spread(n_slot, n_send, n_recv)
+    spread(n_slot, n_send, n_line, n_recv)
 
     width = 256 if Dq % 256 == 0 else 128
 
@@ -218,7 +243,7 @@
         return remote(big.at[p_slot(other(k)), :], yrecv.at[k], y_send.at[k], y_recv.at[k], "mlp", partner)
 
     def z_copy(k):
-        return remote(big.at[p_slot(peer(k)), :], zrecv.at[k - 1], z_send.at[k], z_recv.at[k], "mlp", peer(k))
+        return remote(big.at[p_slot(peer(k)), :], zrecv.at[a], z_send.at[k], z_recv.at[a], "mlp", peer(k))
 
     def combine(k):
         y_copy(k).wait_recv()
@@ -226,31 +251,33 @@
         big[rows, :] = (big[rows, :].astype(jnp.float32) + yrecv[k].astype(jnp.float32)).astype(jnp.bfloat16)
         send(z_copy(k))
 
-    forward_weight(0)
-    forward_weight(1)
+    for k in range(1, A - 1):
+        forward(k, n_slot, n_send, n_line, n_recv)
+    for i in range(3):
+        forward_weight(i)
     if A > 1:
-        forward(1, n_slot, n_recv, n_fwd)
-    forward_weight(2)
+        forward(A - 1, n_slot, n_send, n_line, n_recv)
     for i in range(3):
         weight_arrived(i)
-    for k in range(A):
-        arrived(n_slot, other(k), n_recv, n_fwd)
-        feed(flip(a, k))
+    order = [*range(1, A), 0]
+    for i, k in enumerate(order):
+        arrived(n_slot, other(k), n_recv)
+        feed(nearest(a, A, k))
         send(y_copy(k))
-        if k + 2 < A:
-            forward(k + 2, n_slot, n_recv, n_fwd)
-        if k >= 2:
-            combine(k - 1)
-    if A > 1:
-        combine(A - 1)
+        if i:
+            combine(order[i - 1])
     y_copy(0).wait_recv()
     h[...] = h[...] + (big[p_slot(me), :].astype(jnp.float32) + yrecv[0].astype(jnp.float32))
     for k in range(1, A):
-        z_copy(k).wait_recv()
-        h[...] = h[...] + zrecv[k - 1].astype(jnp.float32)
+        s = nearest(a, A, k)
+        remote(zrecv.at[s], zrecv.at[s], z_send.at[k], z_recv.at[s], "mlp", partner).wait_recv()
+        h[...] = h[...] + zrecv[s].astype(jnp.float32)
     out_ref[...] = h[...].astype(jnp.bfloat16)
-    for copy in started:
-        copy.wait_send()
+    for copy, when in started:
+        if when is None:
+            copy.wait_send()
+        else:
+            pl.when(when)(copy.wait_send)
 
 
 def body(
@@ -290,14 +317,14 @@
             pltpu.VMEM((nr, F, Dq), bf16),
             pltpu.VMEM((max(n * T, out_weight.shape[0]), D), bf16),
             pltpu.VMEM((A, T, D), bf16),
-            pltpu.VMEM((A - 1, T, D), bf16),
+            pltpu.VMEM((A, T, D), bf16),
             pltpu.VMEM((T, D), f32),
             pltpu.VMEM((T, QUERY_HEADS * HEAD_SIZE), bf16),
             pltpu.VMEM((T, n * R), f32),
             pltpu.VMEM((2 * T, F), bf16),
             dma((8,)),
-            dma((A,)), dma((A,)), dma((n,)),
-            dma((A,)), dma((A,)), dma((n,)),
+            dma((A,)), dma((A + 1,)), dma((n,)),
+            dma((A,)), dma((A + 1,)), dma((n,)),
             dma((3, X)), dma((3, X)), dma((3, nr)),
             dma((A,)), dma((A,)), dma((A,)), dma((A,)),
         ],

time: 279 us -> 236 us (0.85)
  the two profiles are of different devices: /device:TPU:9 before, /device:TPU:0 now
where the time goes in v2:
time: 236 us
  Pallas kernels  231 us (98%)
  local copies, waits for them, and re-layouts  3.04 us (1%)
    pallas_call x1, Pallas kernels, body(): pl.pallas_call(functools.partial(kernel, n, nr), out_shape=jax.ShapeDtype...  231 us

profile of v2, /device:TPU:0, one launch (start us, length us, event | category | flops | bytes accessed | tf_op | source)
XLA Modules:
  0.0 236.2 jit_solution(9572328103596478684)
XLA Ops:
  0.7 0.8 select_reduce_fusion
  1.4 0.8 fusion.1
  2.2 0.1 and.13
  2.3 0.1 copy.18
  2.4 0.1 mul.12
  2.5 0.1 copy.19
  2.6 0.1 fusion.3
  2.6 0.6 copy.20
  3.3 230.8 %shard_map.127 = bf16[128,3072]{1,0:T(8,128)(2,1)} custom-call(bf16[128,1536]{1,0:T(8,128)(2,1)} %q_ref.1, bf16[128,3072]{1,0:T(8,128)(2,1)} %resid_ref.1, s32[1,3072]{1,0:T(1,128)} %bitcast.24, f32[1,3072]{1,0:T(1,128)} %bitcast.25, bf16[128,256]{1,0:T(8,128)(2,1)} %fk.1, bf16[128,256]{1,0:T(8,128)(2,1)} %fv.1, bf16[256,256]{1,0:T(8,128)(2,1)} %bitcast.22, ...), custom_call_target="tpu_custom_call" | custom-call | tf_op jit(solution)/shard_map/pallas_call | solution.py:307
  234.1 2.1 copy.23
  (4 shorter events, 0.0 us)

commit v3 on v2

--- a/solution.py
+++ b/solution.py
@@ -143,9 +143,12 @@
         return nearest(a, A, k) * 2 + 1 - b
 
     spread(kv_slot, kv_send, kv_line, kv_recv)
-    for i in range(3):
+    def weight_out(i):
         for k in range(1, X):
             send(remote(weights[i], w_slot(i, r), w_send.at[i, k], w_recv.at[i, r], "req", rpeer(k)))
+
+    weight_out(0)
+    weight_out(1)
     for i in range(3):
         send(remote(weights[i], w_slot(i, r), w_send.at[i, 0], w_recv.at[i, r], "req", sibling))
     own_ow.start()
@@ -170,6 +173,7 @@
         forward(k, kv_slot, kv_send, kv_line, kv_recv)
     for k in range(A):
         arrived(kv_slot, other(k), kv_recv)
+    weight_out(2)
 
     factor = HEAD_SIZE ** (-0.5) * math.log2(math.e)
 
@@ -213,7 +217,7 @@
 
     width = 256 if Dq % 256 == 0 else 128
 
-    def feed(ap):
+    def feed(ap, wait, out):
         pair = pl.ds(pl.multiple_of(ap * 2 * T, 256), 2 * T)
 
         def gated(j, carry):
@@ -223,7 +227,12 @@
             hid[:, cols] = (gate / (1.0 + jnp.exp(-gate)) * upper).astype(jnp.bfloat16)
             return carry
 
+        if wait:
+            weight_arrived(0)
+            weight_arrived(1)
         lax.fori_loop(0, F // 256, gated, 0)
+        if wait:
+            weight_arrived(2)
 
         def lowered(s, carry):
             for j in range(Dq // width):
@@ -234,22 +243,36 @@
                 big[pair, cols] = piece.astype(jnp.bfloat16)
             return carry
 
-        lax.fori_loop(0, nr, lowered, 0)
+        lax.fori_loop(0, nr // 2, lowered, 0)
+        out(0)
+        lax.fori_loop(nr // 2, nr, lowered, 0)
+        out(1)
 
     def p_slot(s):
         return pl.ds(pl.multiple_of(s * T, 128), T)
 
-    def y_copy(k):
-        return remote(big.at[p_slot(other(k)), :], yrecv.at[k], y_send.at[k], y_recv.at[k], "mlp", partner)
-
-    def z_copy(k):
-        return remote(big.at[p_slot(peer(k)), :], zrecv.at[a], z_send.at[k], z_recv.at[a], "mlp", peer(k))
+    halves = (pl.ds(0, D // 2), pl.ds(D // 2, D // 2))
+
+    def y_copy(k, f):
+        return remote(
+            big.at[p_slot(other(k)), halves[f]], yrecv.at[k, :, halves[f]],
+            y_send.at[k, f], y_recv.at[k, f], "mlp", partner,
+        )
+
+    def z_copy(k, f):
+        return remote(
+            big.at[p_slot(peer(k)), halves[f]], zrecv.at[a, :, halves[f]],
+            z_send.at[k, f], z_recv.at[a, f], "mlp", peer(k),
+        )
 
     def combine(k):
-        y_copy(k).wait_recv()
         rows = p_slot(peer(k))
-        big[rows, :] = (big[rows, :].astype(jnp.float32) + yrecv[k].astype(jnp.float32)).astype(jnp.bfloat16)
-        send(z_copy(k))
+        for f, cols in enumerate(halves):
+            y_copy(k, f).wait_recv()
+            big[rows, cols] = (
+                big[rows, cols].astype(jnp.float32) + yrecv[k, :, cols].astype(jnp.float32)
+            ).astype(jnp.bfloat16)
+            send(z_copy(k, f))
 
     for k in range(1, A - 1):
         forward(k, n_slot, n_send, n_line, n_recv)
@@ -257,21 +280,23 @@
         forward_weight(i)
     if A > 1:
         forward(A - 1, n_slot, n_send, n_line, n_recv)
-    for i in range(3):
-        weight_arrived(i)
-    order = [*range(1, A), 0]
+    order = [*range(A - 1, 0, -1), 0]
     for i, k in enumerate(order):
         arrived(n_slot, other(k), n_recv)
-        feed(nearest(a, A, k))
-        send(y_copy(k))
+        feed(nearest(a, A, k), i == 0, lambda f: send(y_copy(k, f)))
         if i:
             combine(order[i - 1])
-    y_copy(0).wait_recv()
-    h[...] = h[...] + (big[p_slot(me), :].astype(jnp.float32) + yrecv[0].astype(jnp.float32))
-    for k in range(1, A):
+    for f, cols in enumerate(halves):
+        y_copy(0, f).wait_recv()
+        h[:, cols] = h[:, cols] + (
+            big[p_slot(me), cols].astype(jnp.float32) + yrecv[0, :, cols].astype(jnp.float32)
+        )
+    for k in order[:-1]:
         s = nearest(a, A, k)
-        remote(zrecv.at[s], zrecv.at[s], z_send.at[k], z_recv.at[s], "mlp", partner).wait_recv()
-        h[...] = h[...] + zrecv[s].astype(jnp.float32)
+        for f, cols in enumerate(halves):
+            here = zrecv.at[s, :, cols]
+            remote(here, here, z_send.at[k, f], z_recv.at[s, f], "mlp", partner).wait_recv()
+            h[:, cols] = h[:, cols] + zrecv[s, :, cols].astype(jnp.float32)
     out_ref[...] = h[...].astype(jnp.bfloat16)
     for copy, when in started:
         if when is None:
@@ -326,7 +351,7 @@
             dma((A,)), dma((A + 1,)), dma((n,)),
             dma((A,)), dma((A + 1,)), dma((n,)),
             dma((3, X)), dma((3, X)), dma((3, nr)),
-            dma((A,)), dma((A,)), dma((A,)), dma((A,)),
+            dma((A, 2)), dma((A, 2)), dma((A, 2)), dma((A, 2)),
         ],
         compiler_params=pltpu.CompilerParams(
             collective_id=0, has_side_effects=True, vmem_limit_bytes=62 * 2**20

time: 236 us -> 224 us (0.949)
  Pallas kernels: 231 us -> 219 us
    pallas_call x1, Pallas kernels: 231 us -> 219 us  [body(): pl.pallas_call(functools.partial(kernel, n, nr), out_shape=jax.ShapeDtype...]
where the time goes in v3:
time: 224 us
  Pallas kernels  219 us (98%)
  local copies, waits for them, and re-layouts  3.04 us (1%)
    pallas_call x1, Pallas kernels, body(): pl.pallas_call(functools.partial(kernel, n, nr), out_shape=jax.ShapeDtype...  219 us

profile of v3, /device:TPU:0, one launch (start us, length us, event | category | flops | bytes accessed | tf_op | source)
XLA Modules:
  0.0 223.9 jit_solution(6540444250832956305)
XLA Ops:
  0.7 0.8 select_reduce_fusion
  1.4 0.8 fusion.1
  2.2 0.1 and.13
  2.3 0.1 copy.18
  2.4 0.1 mul.12
  2.5 0.1 copy.19
  2.6 0.1 fusion.3
  2.6 0.6 copy.20
  3.3 218.5 %shard_map.127 = bf16[128,3072]{1,0:T(8,128)(2,1)} custom-call(bf16[128,1536]{1,0:T(8,128)(2,1)} %q_ref.1, bf16[128,3072]{1,0:T(8,128)(2,1)} %resid_ref.1, s32[1,3072]{1,0:T(1,128)} %bitcast.24, f32[1,3072]{1,0:T(1,128)} %bitcast.25, bf16[128,256]{1,0:T(8,128)(2,1)} %fk.1, bf16[128,256]{1,0:T(8,128)(2,1)} %fv.1, bf16[256,256]{1,0:T(8,128)(2,1)} %bitcast.22, ...), custom_call_target="tpu_custom_call" | custom-call | tf_op jit(solution)/shard_map/pallas_call | solution.py:332
  221.8 2.1 copy.23
  (4 shorter events, 0.0 us)
